TPU v7x, 32 devices: a whole 2x2x4 slice. The times are simulated.
32 devices in a mesh: dp: 16 (over z, x, core), tensor: 2 (over y).
Axes of the slice: x: 2, y: 2, z: 4, core: 2. Of those that a mesh axis runs over, the one named last changes fastest.
Arguments:
- tokens: bfloat16 [16, 736, 1152], P('dp', 'tensor'), may hold values from -6 to 6
- cotangent: bfloat16 [16, 736, 1152], P('dp', 'tensor'), may hold values from -6 to 6
- counts: int32 [16], P('dp'), may hold values from 638 to 729
- joint_weight: float32 [1152, 3, 1152], P('dp', None, 'tensor'), may hold values from -0.1875 to 0.1875
- joint_moment: float32 [1152, 3, 1152], P('dp', None, 'tensor'), may hold values from -0.0014648438 to 0.0014648438
- joint_square: float32 [1152, 3, 1152], P('dp', None, 'tensor'), may hold values from 4.53793e-09 to 3.630344e-08
- output_weight: float32 [1152, 1152], P('tensor', 'dp'), may hold values from -0.5 to 0.5
- output_moment: float32 [1152, 1152], P('tensor', 'dp'), may hold values from -0.0029296875 to 0.0029296875
- output_square: float32 [1152, 1152], P('tensor', 'dp'), may hold values from 1.815172e-08 to 1.4521376e-07
- expand_weight: float32 [1152, 4304], P('dp', 'tensor'), may hold values from -0.1875 to 0.1875
- expand_moment: float32 [1152, 4304], P('dp', 'tensor'), may hold values from -0.0029296875 to 0.0029296875
- expand_square: float32 [1152, 4304], P('dp', 'tensor'), may hold values from 1.815172e-08 to 1.4521376e-07
- reduce_weight: float32 [4304, 1152], P('tensor', 'dp'), may hold values from -0.09375 to 0.09375
- reduce_moment: float32 [4304, 1152], P('tensor', 'dp'), may hold values from -0.005859375 to 0.005859375
- reduce_square: float32 [4304, 1152], P('tensor', 'dp'), may hold values from 7.260688e-08 to 5.8085504e-07
- norm_gains: float32 [2, 1152], replicated, may hold values from 0.5 to 1.5
- gains_moment: float32 [2, 1152], replicated, may hold values from -0.009765625 to 0.009765625
- gains_square: float32 [2, 1152], replicated, may hold values from 2.0168576e-07 to 1.6134861e-06
- shifts: float32 [4, 1152], replicated, may hold values from -3 to 3
- shifts_moment: float32 [4, 1152], replicated, may hold values from -0.009765625 to 0.009765625
- shifts_square: float32 [4, 1152], replicated, may hold values from 2.0168576e-07 to 1.6134861e-06
- head_bias: float32 [2, 1152], P(None, 'tensor'), may hold values from -3 to 3
- head_moment: float32 [2, 1152], P(None, 'tensor'), may hold values from -0.0029296875 to 0.0029296875
- head_square: float32 [2, 1152], P(None, 'tensor'), may hold values from 1.815172e-08 to 1.4521376e-07
- hidden_bias: float32 [4304], P('tensor'), may hold values from -3 to 3
- hidden_moment: float32 [4304], P('tensor'), may hold values from -0.0029296875 to 0.0029296875
- hidden_square: float32 [4304], P('tensor'), may hold values from 1.815172e-08 to 1.4521376e-07
Outputs:
- layer_out: bfloat16 [16, 736, 1152], P('dp', 'tensor')
- input_grad: bfloat16 [16, 736, 1152], P('dp', 'tensor')
- grad_norm: float32 [], replicated
- joint_new: float32 [1152, 3, 1152], P('dp', None, 'tensor')
- joint_moment_new: float32 [1152, 3, 1152], P('dp', None, 'tensor')
- joint_square_new: float32 [1152, 3, 1152], P('dp', None, 'tensor')
- joint_copy: bfloat16 [1152, 3, 1152], P('dp', None, 'tensor')
- output_new: float32 [1152, 1152], P('tensor', 'dp')
- output_moment_new: float32 [1152, 1152], P('tensor', 'dp')
- output_square_new: float32 [1152, 1152], P('tensor', 'dp')
- output_copy: bfloat16 [1152, 1152], P('tensor', 'dp')
- expand_new: float32 [1152, 4304], P('dp', 'tensor')
- expand_moment_new: float32 [1152, 4304], P('dp', 'tensor')
- expand_square_new: float32 [1152, 4304], P('dp', 'tensor')
- expand_copy: bfloat16 [1152, 4304], P('dp', 'tensor')
- reduce_new: float32 [4304, 1152], P('tensor', 'dp')
- reduce_moment_new: float32 [4304, 1152], P('tensor', 'dp')
- reduce_square_new: float32 [4304, 1152], P('tensor', 'dp')
- reduce_copy: bfloat16 [4304, 1152], P('tensor', 'dp')
- gains_new: float32 [2, 1152], replicated
- gains_moment_new: float32 [2, 1152], replicated
- gains_square_new: float32 [2, 1152], replicated
- shifts_new: float32 [4, 1152], replicated
- shifts_moment_new: float32 [4, 1152], replicated
- shifts_square_new: float32 [4, 1152], replicated
- head_new: float32 [2, 1152], P(None, 'tensor')
- head_moment_new: float32 [2, 1152], P(None, 'tensor')
- head_square_new: float32 [2, 1152], P(None, 'tensor')
- hidden_new: float32 [4304], P('tensor')
- hidden_moment_new: float32 [4304], P('tensor')
- hidden_square_new: float32 [4304], P('tensor')
Inputs may be any that keep to these rules, and one draw needn't show every extreme that they name: `counts`: valid tokens of each image; key slots from there up to 736 are padding.
All inputs are finite; a program needn't handle non-finite values.
Results may differ from a plain program's by a relative error of at most 0.01.
Values may be sent and summed in bfloat16 or wider, within the bound.
A program may use at most 192 MiB of HBM per device.

v0:
```python
import jax
import jax.numpy as jnp
from jax import lax
from jax.sharding import PartitionSpec as P

HD = 72
STEP = 4
norm_eps = 1e-06
clip_limit = 1.0
matrix_rate = 0.03
vector_rate = 0.3
decay_rate = 0.1
adam_eps = 1e-08
mask_fill = -1e30


def layer_norm(values, gain, shift):
    center = jnp.mean(values, axis=-1, keepdims=True)
    centred = values - center
    spread = jnp.mean(centred * centred, axis=-1, keepdims=True)
    return centred * lax.rsqrt(spread + norm_eps) * gain + shift


def gelu_tanh(values):
    return jax.nn.gelu(values, approximate=True)


def whole_rows(part):
    return lax.all_gather(part, "tensor", axis=1, tiled=True)


def share_rows(full):
    return lax.psum_scatter(
        full.astype(jnp.bfloat16), "tensor", scatter_dimension=1, tiled=True
    ).astype(jnp.float32)


def scatter_sum(part, dim):
    return lax.psum_scatter(
        part.astype(jnp.bfloat16), "dp", scatter_dimension=dim, tiled=True
    ).astype(jnp.float32)


def split_heads(joint):
    length = joint.shape[0]
    heads_local = joint.shape[2] // HD
    query = joint[:, 0].reshape(length, heads_local, HD)
    keys = joint[:, 1].reshape(length, heads_local, HD)
    values = joint[:, 2].reshape(length, heads_local, HD)
    return (query, keys, values)


def masked_scores(query, keys, count):
    length = query.shape[0]
    scores = jnp.einsum("qhd,khd->hqk", query, keys, preferred_element_type=jnp.float32) * HD ** (
        -0.5
    )
    valid = jnp.arange(length, dtype=jnp.int32) < count
    return jnp.where(valid[None, None, :], scores, mask_fill)


def attend(joint, count):
    query, keys, values = split_heads(joint)
    scores = masked_scores(query, keys, count)
    top = jnp.max(scores, axis=-1, keepdims=True)
    total = jnp.sum(jnp.exp(scores - top), axis=-1, keepdims=True)
    logsum = top + jnp.log(total)
    probs = jnp.exp(scores - logsum)
    mixed = jnp.einsum(
        "hqk,khd->qhd", probs.astype(jnp.bfloat16), values, preferred_element_type=jnp.float32
    )
    return (mixed.reshape(joint.shape[0], joint.shape[2]).astype(jnp.bfloat16), logsum[:, :, 0])


def attend_back(joint, mixed_grad, logsum, count):
    query, keys, values = split_heads(joint)
    length = joint.shape[0]
    grad_heads = mixed_grad.reshape(length, joint.shape[2] // HD, HD)
    scores = masked_scores(query, keys, count)
    probs = jnp.exp(scores - logsum[:, :, None])
    value_grad = jnp.einsum(
        "hqk,qhd->khd", probs.astype(jnp.bfloat16), grad_heads, preferred_element_type=jnp.float32
    )
    prob_grad = jnp.einsum("qhd,khd->hqk", grad_heads, values, preferred_element_type=jnp.float32)
    inner = jnp.sum(probs * prob_grad, axis=-1, keepdims=True)
    score_grad = (probs * (prob_grad - inner)).astype(jnp.bfloat16)
    query_grad = jnp.einsum(
        "hqk,khd->qhd", score_grad, keys, preferred_element_type=jnp.float32
    ) * HD ** (-0.5)
    key_grad = jnp.einsum(
        "hqk,qhd->khd", score_grad, query, preferred_element_type=jnp.float32
    ) * HD ** (-0.5)
    stacked = jnp.stack([query_grad, key_grad, value_grad], axis=1)
    return stacked.reshape(length, 3, joint.shape[2]).astype(jnp.bfloat16)


def forward_pass(tokens, counts, weights, small):
    joint_w, expand_w, output_w, reduce_w = weights
    norm_gains, shifts, head_bias, hidden_bias = small
    rows = tokens.astype(jnp.float32)
    normed, first_back = jax.vjp(layer_norm, rows, norm_gains[0], shifts[0])
    normed_whole = whole_rows(normed.astype(jnp.bfloat16))
    joint = jnp.einsum("bsd,dch->bsch", normed_whole, joint_w, preferred_element_type=jnp.float32)
    bias = jnp.stack([head_bias[0], jnp.zeros_like(head_bias[0]), head_bias[1]])
    joint = (joint + bias).astype(jnp.bfloat16)
    mixed, logsum = lax.map(lambda pair: attend(pair[0], pair[1]), (joint, counts))
    branch = (
        share_rows(jnp.einsum("bsh,hd->bsd", mixed, output_w, preferred_element_type=jnp.float32))
        + shifts[2]
    )
    middle = rows + branch
    second, second_back = jax.vjp(layer_norm, middle, norm_gains[1], shifts[1])
    second_whole = whole_rows(second.astype(jnp.bfloat16))
    before = (
        jnp.einsum("bsd,df->bsf", second_whole, expand_w, preferred_element_type=jnp.float32)
        + hidden_bias
    )
    active, gelu_back = jax.vjp(gelu_tanh, before)
    active = active.astype(jnp.bfloat16)
    result = (
        share_rows(jnp.einsum("bsf,fd->bsd", active, reduce_w, preferred_element_type=jnp.float32))
        + shifts[3]
    )
    saved = (
        first_back,
        normed_whole,
        joint,
        mixed,
        logsum,
        second_back,
        second_whole,
        active,
        gelu_back,
    )
    return (middle + result, saved)


def adamw_step(weight, grad, moment, square, factor, rate, decay):
    clipped = grad * factor
    moment_new = 0.5 * moment + 0.5 * clipped
    square_new = 0.5 * square + 0.5 * clipped * clipped
    correct = 1.0 - 0.5**STEP
    update = moment_new / correct / (jnp.sqrt(square_new / correct) + adam_eps)
    return (weight - rate * (update + decay * weight), moment_new, square_new)


def squares(values):
    return jnp.sum(values * values)


def on_device(
    tokens,
    cotangent,
    counts,
    joint_weight,
    joint_moment,
    joint_square,
    output_weight,
    output_moment,
    output_square,
    expand_weight,
    expand_moment,
    expand_square,
    reduce_weight,
    reduce_moment,
    reduce_square,
    norm_gains,
    gains_moment,
    gains_square,
    shifts,
    shifts_moment,
    shifts_square,
    head_bias,
    head_moment,
    head_square,
    hidden_bias,
    hidden_moment,
    hidden_square,
):
    first_pair = (
        lax.all_gather(joint_weight.astype(jnp.bfloat16), "dp", axis=0, tiled=True),
        lax.all_gather(expand_weight.astype(jnp.bfloat16), "dp", axis=0, tiled=True),
    )
    second_pair = (
        lax.all_gather(output_weight.astype(jnp.bfloat16), "dp", axis=1, tiled=True),
        lax.all_gather(reduce_weight.astype(jnp.bfloat16), "dp", axis=1, tiled=True),
    )
    weights = (first_pair[0], first_pair[1], second_pair[0], second_pair[1])
    small = (norm_gains, shifts, head_bias, hidden_bias)
    layer_rows, saved = forward_pass(tokens, counts, weights, small)
    layer_out = layer_rows.astype(jnp.bfloat16)
    first_back, normed_whole, joint, mixed, logsum, second_back, second_whole, active, gelu_back = (
        saved
    )
    joint_w, expand_w, output_w, reduce_w = weights
    grad_rows = cotangent.astype(jnp.float32)
    grad_whole = whole_rows(cotangent)
    reduce_grad = jnp.einsum("bsf,bsd->fd", active, grad_whole, preferred_element_type=jnp.float32)
    active_grad = jnp.einsum(
        "bsd,fd->bsf", grad_whole, reduce_w, preferred_element_type=jnp.float32
    )
    before_grad = gelu_back(active_grad)[0].astype(jnp.bfloat16)
    expand_grad = jnp.einsum(
        "bsd,bsf->df", second_whole, before_grad, preferred_element_type=jnp.float32
    )
    hidden_grad = jnp.sum(before_grad, axis=(0, 1), dtype=jnp.float32)
    second_grad = share_rows(
        jnp.einsum("bsf,df->bsd", before_grad, expand_w, preferred_element_type=jnp.float32)
    )
    middle_part, gain_two, shift_two = second_back(second_grad)
    middle_grad = grad_rows + middle_part
    branch_grad = middle_grad.astype(jnp.bfloat16)
    branch_whole = whole_rows(branch_grad)
    output_grad = jnp.einsum("bsh,bsd->hd", mixed, branch_whole, preferred_element_type=jnp.float32)
    mixed_grad = jnp.einsum(
        "bsd,hd->bsh", branch_whole, output_w, preferred_element_type=jnp.float32
    ).astype(jnp.bfloat16)
    joint_grad = lax.map(
        lambda group: attend_back(group[0], group[1], group[2], group[3]),
        (joint, mixed_grad, logsum, counts),
    )
    joint_weight_grad = jnp.einsum(
        "bsd,bsch->dch", normed_whole, joint_grad, preferred_element_type=jnp.float32
    )
    head_grad = jnp.sum(joint_grad[:, :, 0::2], axis=(0, 1), dtype=jnp.float32)
    first_grad = share_rows(
        jnp.einsum("bsch,dch->bsd", joint_grad, joint_w, preferred_element_type=jnp.float32)
    )
    rows_part, gain_one, shift_one = first_back(first_grad)
    input_grad = (middle_grad + rows_part).astype(jnp.bfloat16)
    gain_grad = jnp.stack([gain_one, gain_two])
    shift_grad = jnp.stack(
        [
            shift_one,
            shift_two,
            jnp.sum(branch_grad, axis=(0, 1), dtype=jnp.float32),
            jnp.sum(grad_rows, axis=(0, 1)),
        ]
    )
    joint_sum, expand_sum = (scatter_sum(joint_weight_grad, 0), scatter_sum(expand_grad, 0))
    output_sum, reduce_sum = (scatter_sum(output_grad, 1), scatter_sum(reduce_grad, 1))
    gain_sum, shift_sum = lax.psum((gain_grad, shift_grad), ("dp", "tensor"))
    head_sum, hidden_sum = lax.psum((head_grad, hidden_grad), "dp")
    data_count = lax.axis_size("dp")
    split_count = lax.axis_size("tensor")
    owned = squares(joint_sum) + squares(expand_sum) + squares(output_sum) + squares(reduce_sum)
    shared = (squares(head_sum) + squares(hidden_sum)) / data_count
    everywhere = (squares(gain_sum) + squares(shift_sum)) / (data_count * split_count)
    grad_norm = jnp.sqrt(lax.psum(owned + shared + everywhere, ("dp", "tensor")))
    factor = clip_limit / jnp.maximum(grad_norm, clip_limit)
    joint_state = adamw_step(
        joint_weight, joint_sum, joint_moment, joint_square, factor, matrix_rate, decay_rate
    )
    output_state = adamw_step(
        output_weight, output_sum, output_moment, output_square, factor, matrix_rate, decay_rate
    )
    expand_state = adamw_step(
        expand_weight, expand_sum, expand_moment, expand_square, factor, matrix_rate, decay_rate
    )
    reduce_state = adamw_step(
        reduce_weight, reduce_sum, reduce_moment, reduce_square, factor, matrix_rate, decay_rate
    )
    gains_state = adamw_step(
        norm_gains, gain_sum, gains_moment, gains_square, factor, vector_rate, 0.0
    )
    shifts_state = adamw_step(
        shifts, shift_sum, shifts_moment, shifts_square, factor, vector_rate, 0.0
    )
    head_state = adamw_step(head_bias, head_sum, head_moment, head_square, factor, vector_rate, 0.0)
    hidden_state = adamw_step(
        hidden_bias, hidden_sum, hidden_moment, hidden_square, factor, vector_rate, 0.0
    )
    return (
        layer_out,
        input_grad,
        grad_norm,
        joint_state[0],
        joint_state[1],
        joint_state[2],
        joint_state[0].astype(jnp.bfloat16),
        output_state[0],
        output_state[1],
        output_state[2],
        output_state[0].astype(jnp.bfloat16),
        expand_state[0],
        expand_state[1],
        expand_state[2],
        expand_state[0].astype(jnp.bfloat16),
        reduce_state[0],
        reduce_state[1],
        reduce_state[2],
        reduce_state[0].astype(jnp.bfloat16),
        gains_state[0],
        gains_state[1],
        gains_state[2],
        shifts_state[0],
        shifts_state[1],
        shifts_state[2],
        head_state[0],
        head_state[1],
        head_state[2],
        hidden_state[0],
        hidden_state[1],
        hidden_state[2],
    )


def solution(mesh):
    in_specs = (
        P("dp", "tensor", None),
        P("dp", "tensor", None),
        P("dp"),
        P("dp", None, "tensor"),
        P("dp", None, "tensor"),
        P("dp", None, "tensor"),
        P("tensor", "dp"),
        P("tensor", "dp"),
        P("tensor", "dp"),
        P("dp", "tensor"),
        P("dp", "tensor"),
        P("dp", "tensor"),
        P("tensor", "dp"),
        P("tensor", "dp"),
        P("tensor", "dp"),
        P(),
        P(),
        P(),
        P(),
        P(),
        P(),
        P(None, "tensor"),
        P(None, "tensor"),
        P(None, "tensor"),
        P("tensor"),
        P("tensor"),
        P("tensor"),
    )
    out_specs = (
        P("dp", "tensor", None),
        P("dp", "tensor", None),
        P(),
        P("dp", None, "tensor"),
        P("dp", None, "tensor"),
        P("dp", None, "tensor"),
        P("dp", None, "tensor"),
        P("tensor", "dp"),
        P("tensor", "dp"),
        P("tensor", "dp"),
        P("tensor", "dp"),
        P("dp", "tensor"),
        P("dp", "tensor"),
        P("dp", "tensor"),
        P("dp", "tensor"),
        P("tensor", "dp"),
        P("tensor", "dp"),
        P("tensor", "dp"),
        P("tensor", "dp"),
        P(),
        P(),
        P(),
        P(),
        P(),
        P(),
        P(None, "tensor"),
        P(None, "tensor"),
        P(None, "tensor"),
        P("tensor"),
        P("tensor"),
        P("tensor"),
    )
    return jax.shard_map(
        on_device, mesh=mesh, in_specs=in_specs, out_specs=out_specs, check_vma=False
    )
```

profile of v0, /device:TPU:0, one launch (start us, length us, event | category | flops | bytes accessed | tf_op | source)
XLA Modules:
  0.0 853.5 jit_solution(2574007469518018370)
XLA Ops:
  17.5 29.0 %all-gather.9.cloned.1.call-done = bf16[1,736,1152]{2,1,0:T(8,128)(2,1)} async-done(((bf16[1,368,1152]{2,1,0:T(8,128)(2,1)}), bf16[1,736,1152]{2,1,0:T(8,128)(2,1)}) %all-gather.9.cloned.1.call-update) | async-done | bytes 1695760 | tf_op jit(solution)/shard_map/all_gather | solution.py:29
  46.5 54.5 %all-gather.11.cloned.1.call-done = bf16[1152,3,576]{2,0,1:T(8,128)(2,1)} async-done(((bf16[72,3,576]{2,0,1:T(8,128)(2,1)}), bf16[1152,3,576]{2,0,1:T(8,128)(2,1)}) %all-gather.11.cloned.1.call-update) | async-done | bytes 3981328 | tf_op jit(solution)/shard_map/all_gather | solution.py:181
  101.0 6.4 add_convert_fusion
  107.7 8.6 %fusion = (f32[8,736]{1,0:T(8,128)S(1)}, f32[8,736,736]{1,2,0:T(8,128)}) fusion(pred[736]{0:T(1024)(128)(4,1)S(1)} %iota_compare_fusion, bf16[736,8,72]{0,2,1:T(8,128)(2,1)S(1)} %bitcast.96, bf16[736,8,72]{0,2,1:T(8,128)(2,1)S(1)} %bitcast.94), kind=kOutput, calls=%fused_computation.5 | convolution fusion | flops 637028608 | bytes 19054304 | tf_op jit(solution)/shard_map/while/body/eval_jaxpr/qhd,khd->hqk/dot_general | solution.py:55
  116.3 10.0 %exponential_reduce_fusion = f32[8,736]{1,0:T(8,128)S(1)} fusion(f32[8,736,736]{1,2,0:T(8,128)} %get-tuple-element.122, f32[8,736]{1,0:T(8,128)S(1)} %get-tuple-element.121, pred[736]{0:T(1024)(128)(4,1)S(1)} %iota_compare_fusion), kind=kLoop, calls=%fused_computation.3 | loop fusion | flops 17328384 | bytes 17382112 | tf_op jit(solution)/shard_map/while/body/eval_jaxpr/reduce_sum | solution.py:66
  126.3 8.2 fusion.1
  146.9 25.5 %reduce-scatter.17.cloned.1.call-done = bf16[1,368,1152]{2,1,0:T(8,128)(2,1)} async-done(((bf16[1,736,1152]{2,1,0:T(8,128)(2,1)}), bf16[1,368,1152]{2,1,0:T(8,128)(2,1)}) %reduce-scatter.17.cloned.1.call-update) | async-done | bytes 847888 | tf_op jit(solution)/shard_map/reduce_scatter | solution.py:33
  179.3 50.8 %all-gather.17.cloned.1.call-done = bf16[1152,2152]{1,0:T(8,128)(2,1)} async-done(((bf16[72,2152]{1,0:T(8,128)(2,1)}), bf16[1152,2152]{1,0:T(8,128)(2,1)}) %all-gather.17.cloned.1.call-update) | async-done | bytes 4958224 | tf_op jit(solution)/shard_map/all_gather | solution.py:182
  230.1 29.2 %all-gather.15.cloned.1.call-done = bf16[1,736,1152]{2,1,0:T(8,128)(2,1)} async-done(((bf16[1,368,1152]{2,1,0:T(8,128)(2,1)}), bf16[1,736,1152]{2,1,0:T(8,128)(2,1)}) %all-gather.15.cloned.1.call-update) | async-done | bytes 1695760 | tf_op jit(solution)/shard_map/all_gather | solution.py:29
  259.4 10.1 %fusion.38 = f32[736,2152]{1,0:T(8,128)} fusion(bf16[1152,2152]{1,0:T(8,128)(2,1)} %all-gather.17.cloned.1.call-done, bf16[1,736,1152]{2,1,0:T(8,128)(2,1)} %all-gather.15.cloned.1.call-done), kind=kOutput, calls=%fused_computation.72 | convolution fusion | flops 3649241088 | bytes 12989440 | tf_op jit(solution)/shard_map/bsd,df->bsf/dot_general | solution.py:115
  269.5 20.1 %all-gather.21.cloned.1.call-done = bf16[1,736,1152]{2,1,0:T(8,128)(2,1)} async-done(((bf16[1,368,1152]{2,1,0:T(8,128)(2,1)}), bf16[1,736,1152]{2,1,0:T(8,128)(2,1)}) %all-gather.21.cloned.1.call-update) | async-done | bytes 1695760 | tf_op jit(solution)/shard_map/all_gather | solution.py:29
  289.6 57.9 %all-gather.19.cloned.1.call-done = bf16[2152,1152]{0,1:T(8,128)(2,1)} async-done(((bf16[2152,72]{0,1:T(8,128)(2,1)}), bf16[2152,1152]{0,1:T(8,128)(2,1)}) %all-gather.19.cloned.1.call-update) | async-done | bytes 4958224 | tf_op jit(solution)/shard_map/all_gather | solution.py:186
  347.5 11.3 %convert_reduce_fusion = (f32[2152]{0:T(1024)S(1)}, bf16[736,2152]{1,0:T(8,128)(2,1)S(1)}) fusion(f32[736,2152]{1,0:T(8,128)} %fusion.38, f32[2152]{0:T(1024)S(1)} %copy-done.46, bf16[2152,1152]{0,1:T(8,128)(2,1)} %all-gather.19.cloned.1.call-done, bf16[1,736,1152]{2,1,0:T(8,128)(2,1)} %all-gather.21.cloned.1.call-done), kind=kOutput, calls=%fused_computation.18 | convolution fusion | flops 3685668096 | bytes 16174400 | tf_op jit(solution)/shard_map/bsd,fd->bsf/dot_general | solution.py:199
  360.5 8.2 fusion.13
  368.9 11.1 %fusion.12 = bf16[1,736,1152]{2,1,0:T(8,128)(2,1)} fusion(bf16[2152,1152]{0,1:T(8,128)(2,1)} %all-gather.19.cloned.1.call-done, f32[736,2152]{1,0:T(8,128)} %fusion.38, f32[2152]{0:T(1024)S(1)} %copy-done.46), kind=kOutput, calls=%fused_computation.31 | convolution fusion | flops 3665927680 | bytes 12998048 | tf_op jit(solution)/shard_map/bsf,fd->bsd/dot_general | solution.py:121
  380.1 14.7 %reduce-scatter.21.cloned.1.call-done = bf16[1,368,1152]{2,1,0:T(8,128)(2,1)} async-done(((bf16[1,736,1152]{2,1,0:T(8,128)(2,1)}), bf16[1,368,1152]{2,1,0:T(8,128)(2,1)}) %reduce-scatter.21.cloned.1.call-update) | async-done | bytes 847888 | tf_op jit(solution)/shard_map/reduce_scatter | solution.py:33
  396.8 27.5 %reduce-scatter.19.cloned.1.call-done = bf16[1,368,1152]{2,1,0:T(8,128)(2,1)} async-done(((bf16[1,736,1152]{2,1,0:T(8,128)(2,1)}), bf16[1,368,1152]{2,1,0:T(8,128)(2,1)}) %reduce-scatter.19.cloned.1.call-update) | async-done | bytes 847888 | tf_op jit(solution)/shard_map/reduce_scatter | solution.py:33
  429.0 28.7 %all-gather.23.cloned.1.call-done = bf16[1,736,1152]{2,1,0:T(8,128)(2,1)} async-done(((bf16[1,368,1152]{2,1,0:T(8,128)(2,1)}), bf16[1,736,1152]{2,1,0:T(8,128)(2,1)}) %all-gather.23.cloned.1.call-update) | async-done | bytes 1695760 | tf_op jit(solution)/shard_map/all_gather | solution.py:29
  462.4 10.1 %convolution_convert_fusion = bf16[2152,1152]{0,1:T(8,128)(2,1)} fusion(bf16[1,736,1152]{2,1,0:T(8,128)(2,1)} %all-gather.21.cloned.1.call-done, f32[736,2152]{1,0:T(8,128)} %fusion.38, f32[2152]{0:T(1024)S(1)} %copy-done.46), kind=kOutput, calls=%fused_computation.6 | convolution fusion | flops 3667558912 | bytes 12998048 | tf_op jit(solution)/shard_map/bsf,bsd->fd/dot_general | solution.py:198
  472.6 9.1 %convolution_convert_fusion.1 = bf16[1152,2152]{1,0:T(8,128)(2,1)} fusion(bf16[736,2152]{1,0:T(8,128)(2,1)} %copy-done.47, bf16[1,736,1152]{2,1,0:T(8,128)(2,1)} %all-gather.15.cloned.1.call-done), kind=kOutput, calls=%fused_computation.7 | convolution fusion | flops 3651720192 | bytes 9821696 | tf_op jit(solution)/shard_map/bsd,bsf->df/dot_general | solution.py:203
  485.0 6.4 convolution_convert_fusion.7
  491.4 13.2 %multiply_reduce_fusion = (f32[8,736]{1,0:T(8,128)S(1)}, f32[8,736,736]{1,2,0:T(8,128)}) fusion(f32[8,736,736]{1,2,0:T(8,128)} %get-tuple-element.122, f32[8,736]{1,0:T(8,128)S(1)} %log_add_fusion, pred[736]{0:T(1024)(128)(4,1)S(1)} %iota_compare_fusion, bf16[736,8,72]{0,2,1:T(8,128)(2,1)S(1)} %bitcast.108, bf16[736,8,72]{0,2,1:T(8,128)(2,1)S(1)} %bitcast.93), kind=kOutput, calls=%fused_computation.1 | convolution fusion | flops 645695744 | bytes 36412128 | tf_op jit(solution)/shard_map/while/body/eval_jaxpr/qhd,khd->hqk/dot_general | solution.py:84
  504.6 13.0 %multiply_convert_fusion = bf16[8,736,736]{1,2,0:T(8,128)(2,1)S(1)} fusion(f32[8,736,736]{1,2,0:T(8,128)} %get-tuple-element.124, f32[8,736,736]{1,2,0:T(8,128)} %get-tuple-element.122, f32[8,736]{1,0:T(8,128)S(1)} %get-tuple-element.123, f32[8,736]{1,0:T(8,128)S(1)} %log_add_fusion, pred[736]{0:T(1024)(128)(4,1)S(1)} %iota_compare_fusion), kind=kLoop, calls=%fused_computation | loop fusion | flops 26001408 | bytes 43383520 | tf_op jit(solution)/shard_map/while/body/eval_jaxpr/convert_element_type | solution.py:86
  528.8 6.3 convolution_convert_fusion.2
  535.2 18.2 %copy.70 = bf16[1152,3,576]{2,1,0:T(4,128)(2,1)} copy(bf16[1152,3,576]{2,0,1:T(8,128)(2,1)S(1)} %convolution_convert_fusion.2) | data formatting | bytes 7962624
  553.4 12.4 %reshape.392 = bf16[1152,1728]{1,0:T(8,128)(2,1)} reshape(bf16[1152,3,576]{2,1,0:T(4,128)(2,1)} %copy.70) | data formatting | bytes 7962624
  568.3 62.1 %all-reduce.4 = (f32[2,576]{1,0:T(2,128)S(1)}, f32[2152]{0:T(1024)S(1)}) all-reduce(f32[2,576]{1,0:T(2,128)S(1)} %convert_reduce_fusion.1, f32[2152]{0:T(1024)S(1)} %get-tuple-element.125), channel_id=1, replica_groups=mesh['dp'=16,'tensor'=2] {'dp'}, use_global_device_ids=true, to_apply=%region_24.25 | all-reduce | flops 3304 | bytes 26432 | tf_op jit(solution)/shard_map/psum | solution.py:243
  636.3 47.3 %reduce-scatter.27.cloned.1.call-done = bf16[72,2152]{1,0:T(8,128)(2,1)} async-done(((bf16[1152,2152]{1,0:T(8,128)(2,1)}), bf16[72,2152]{1,0:T(8,128)(2,1)}) %reduce-scatter.27.cloned.1.call-update) | async-done | bytes 309904
  685.4 26.8 %reduce-scatter.23.cloned.1.call-done = bf16[1,368,1152]{2,1,0:T(8,128)(2,1)} async-done(((bf16[1,736,1152]{2,1,0:T(8,128)(2,1)}), bf16[1,368,1152]{2,1,0:T(8,128)(2,1)}) %reduce-scatter.23.cloned.1.call-update) | async-done | bytes 847888 | tf_op jit(solution)/shard_map/reduce_scatter | solution.py:33
  717.9 40.8 %all-reduce.3 = (f32[2,1152]{1,0:T(2,128)S(1)}, f32[4,1152]{1,0:T(4,128)S(1)}) all-reduce(f32[2,1152]{1,0:T(2,128)S(1)} %pad_maximum_fusion.6, f32[4,1152]{1,0:T(4,128)S(1)} %pad_maximum_fusion.4), channel_id=1, replica_groups=mesh['dp'=16,'tensor'=2] {'dp','tensor'}, use_global_device_ids=true, to_apply=%region_31.32 | all-reduce | flops 6912 | bytes 55296 | tf_op jit(solution)/shard_map/psum | solution.py:242
  761.3 27.2 %reduce-scatter.25.cloned.1.call-done = bf16[72,1728]{1,0:T(8,128)(2,1)} async-done(((bf16[1152,1728]{1,0:T(8,128)(2,1)}), bf16[72,1728]{1,0:T(8,128)(2,1)}) %reduce-scatter.25.cloned.1.call-update) | async-done | bytes 248848
  793.0 39.4 %psum.39 = f32[]{:T(128)} all-reduce(f32[]{:T(128)S(6)} %add.313), channel_id=1, replica_groups=mesh['dp'=16,'tensor'=2] {'dp','tensor'}, use_global_device_ids=true, to_apply=%region_39.40 | all-reduce | flops 1 | bytes 8 | tf_op jit(solution)/shard_map/psum | solution.py:249
  (202 shorter events, 86.5 us)
Async XLA Ops:
  7.2 39.3 %all-gather.9.cloned.1.call-start = ((), (), s32[]{:S(2)}) async-start(), calls=%async_computation.8 | async-start | bytes 2543616 | tf_op jit(solution)/shard_map/all_gather | solution.py:29
  8.7 98.8 %copy-start.35 = (f32[368]{0:T(512)}, f32[368]{0:T(512)S(1)}, u32[]{:S(2)}) copy-start(f32[368]{0:T(512)S(1)} %broadcast_multiply_fusion.1) | copy-start | bytes 4420
  10.8 96.6 %copy-start.38 = (f32[368]{0:T(512)}, f32[368]{0:T(512)S(1)}, u32[]{:S(2)}) copy-start(f32[368]{0:T(512)S(1)} %fusion.61) | copy-start | bytes 4420
  11.6 95.8 %copy-start.30 = (f32[1152]{0:T(1024)}, f32[1152]{0:T(1024)S(1)}, u32[]{:S(2)}) copy-start(f32[1152]{0:T(1024)S(1)} %get-tuple-element.75) | copy-start | bytes 13828
  15.0 86.0 %all-gather.11.cloned.1.call-start = ((), (), s32[]{:S(2)}) async-start(), calls=%async_computation.9 | async-start | bytes 4700160 | tf_op jit(solution)/shard_map/all_gather | solution.py:181
  15.9 125.8 %all-gather.13.cloned.1.call-start = ((), (), s32[]{:S(2)}) async-start(), calls=%async_computation.10 | async-start | bytes 1566720 | tf_op jit(solution)/shard_map/all_gather | solution.py:185
  16.6 155.8 %reduce-scatter.17.cloned.1.call-start = ((), (), s32[]{:S(2)}) async-start(), calls=%async_computation.11 | async-start | bytes 2543616 | tf_op jit(solution)/shard_map/reduce_scatter | solution.py:33
  146.0 84.2 %all-gather.17.cloned.1.call-start = ((), (), s32[]{:S(2)}) async-start(), calls=%async_computation.13 | async-start | bytes 5326848 | tf_op jit(solution)/shard_map/all_gather | solution.py:182
  146.8 112.6 %all-gather.15.cloned.1.call-start = ((), (), s32[]{:S(2)}) async-start(), calls=%async_computation.12 | async-start | bytes 2543616 | tf_op jit(solution)/shard_map/all_gather | solution.py:29
  177.2 112.5 %all-gather.21.cloned.1.call-start = ((), (), s32[]{:S(2)}) async-start(), calls=%async_computation.16 | async-start | bytes 2543616 | tf_op jit(solution)/shard_map/all_gather | solution.py:29
  177.9 169.6 %all-gather.19.cloned.1.call-start = ((), (), s32[]{:S(2)}) async-start(), calls=%async_computation.14 | async-start | bytes 5326848 | tf_op jit(solution)/shard_map/all_gather | solution.py:186
  178.7 168.8 %copy-start.46 = (f32[2152]{0:T(1024)S(1)}, f32[2152]{0:T(1024)}, u32[]{:S(2)}) copy-start(f32[2152]{0:T(1024)} %param.51) | copy-start | bytes 25828
  178.8 216.0 %reduce-scatter.21.cloned.1.call-start = ((), (), s32[]{:S(2)}) async-start(), calls=%async_computation.17 | async-start | bytes 2543616 | tf_op jit(solution)/shard_map/reduce_scatter | solution.py:33
  368.7 55.7 %reduce-scatter.19.cloned.1.call-start = ((), (), s32[]{:S(2)}) async-start(), calls=%async_computation.15 | async-start | bytes 2543616 | tf_op jit(solution)/shard_map/reduce_scatter | solution.py:33
  380.0 77.7 %all-gather.23.cloned.1.call-start = ((), (), s32[]{:S(2)}) async-start(), calls=%async_computation.18 | async-start | bytes 2543616 | tf_op jit(solution)/shard_map/all_gather | solution.py:29
  428.9 204.0 %reduce-scatter.29.cloned.1.call-start = ((), (), s32[]{:S(2)}) async-start(), calls=%async_computation.22 | async-start | bytes 1566720
  462.2 172.3 %reduce-scatter.31.cloned.1.call-start = ((), (), s32[]{:S(2)}) async-start(), calls=%async_computation.23 | async-start | bytes 5326848
  472.5 211.1 %reduce-scatter.27.cloned.1.call-start = ((), (), s32[]{:S(2)}) async-start(), calls=%async_computation.21 | async-start | bytes 5326848
  481.7 230.4 %reduce-scatter.23.cloned.1.call-start = ((), (), s32[]{:S(2)}) async-start(), calls=%async_computation.19 | async-start | bytes 2543616 | tf_op jit(solution)/shard_map/reduce_scatter | solution.py:33
  528.6 259.9 %reduce-scatter.25.cloned.1.call-start = ((), (), s32[]{:S(2)}) async-start(), calls=%async_computation.20 | async-start | bytes 4386816
  565.8 146.3 %copy-start.31 = (f32[1152]{0:T(1024)S(1)}, f32[1152]{0:T(1024)}, u32[]{:S(2)}) copy-start(f32[1152]{0:T(1024)} %copy-done.30) | copy-start | bytes 13828
  565.9 146.3 %copy-start.36 = (f32[368]{0:T(512)S(1)}, f32[368]{0:T(512)}, u32[]{:S(2)}) copy-start(f32[368]{0:T(512)} %copy-done.35) | copy-start | bytes 4420
  567.9 146.0 %copy-start.45 = (f32[368]{0:T(512)S(1)}, f32[368]{0:T(512)}, u32[]{:S(2)}) copy-start(f32[368]{0:T(512)} %copy-done.44) | copy-start | bytes 4420
  568.0 146.0 %copy-start.39 = (f32[368]{0:T(512)S(1)}, f32[368]{0:T(512)}, u32[]{:S(2)}) copy-start(f32[368]{0:T(512)} %copy-done.38) | copy-start | bytes 4420
  568.0 148.0 %copy-start.10 = (bf16[1,368,1152]{2,1,0:T(8,128)(2,1)S(1)}, bf16[1,368,1152]{2,1,0:T(8,128)(2,1)}, u32[]{:S(2)}) copy-start(bf16[1,368,1152]{2,1,0:T(8,128)(2,1)} %param.28) | copy-start | bytes 2543620
  716.0 117.2 %copy-start.41 = (f32[2,576]{1,0:T(2,128)S(1)}, f32[2,576]{1,0:T(2,128)}, u32[]{:S(2)}) copy-start(f32[2,576]{1,0:T(2,128)} %param.48) | copy-start | bytes 13828
  716.0 118.5 %copy-start.37 = (f32[2,1152]{1,0:T(2,128)S(1)}, f32[2,1152]{1,0:T(2,128)}, u32[]{:S(2)}) copy-start(f32[2,1152]{1,0:T(2,128)} %param.42) | copy-start | bytes 27652
  716.0 121.2 %copy-start.34 = (f32[4,1152]{1,0:T(4,128)S(1)}, f32[4,1152]{1,0:T(4,128)}, u32[]{:S(2)}) copy-start(f32[4,1152]{1,0:T(4,128)} %param.45) | copy-start | bytes 55300
  716.1 121.2 %copy-start.42 = (f32[4,1152]{1,0:T(4,128)S(1)}, f32[4,1152]{1,0:T(4,128)}, u32[]{:S(2)}) copy-start(f32[4,1152]{1,0:T(4,128)} %param.46) | copy-start | bytes 55300
  716.1 121.2 %copy-start.43 = (f32[4,1152]{1,0:T(4,128)S(1)}, f32[4,1152]{1,0:T(4,128)}, u32[]{:S(2)}) copy-start(f32[4,1152]{1,0:T(4,128)} %param.47) | copy-start | bytes 55300
  759.4 81.7 %copy-start.32 = (f32[576,72]{0,1:T(8,128)S(1)}, f32[576,72]{0,1:T(8,128)}, u32[]{:S(2)}) copy-start(f32[576,72]{0,1:T(8,128)} %param.34) | copy-start | bytes 497668
  759.4 81.7 %copy-start.33 = (f32[576,72]{0,1:T(8,128)S(1)}, f32[576,72]{0,1:T(8,128)}, u32[]{:S(2)}) copy-start(f32[576,72]{0,1:T(8,128)} %param.35) | copy-start | bytes 497668
  (34 other events, 381.3 us)
Sparse Core Ops, SparseCore 0:
  15.2 31.2 all-gather.8
  49.3 51.7 all-gather.10
  103.8 37.8 all-gather.12
  146.1 26.2 reduce-scatter.16
  175.2 54.8 all-gather.16
  232.2 27.1 all-gather.14
  261.0 28.5 all-gather.20
  292.6 54.9 all-gather.18
  368.8 25.9 reduce-scatter.20
  396.9 27.4 reduce-scatter.18
  429.1 28.5 all-gather.22
  462.3 58.7 reduce-scatter.28
  525.6 77.2 reduce-scatter.30
  606.7 76.8 reduce-scatter.26
  685.8 26.2 reduce-scatter.22
  715.9 72.6 reduce-scatter.24
where the time goes:
time: 859 us; the launch traced here: 853 us
  waiting for transfers between devices  442 us (51%)
  blocking collectives  142 us (17%)
  matrix products  124 us (14%)
  other arithmetic  79.5 us (9%)
  local copies, waits for them, and re-layouts  40.6 us (5%)
  between operations  22.6 us (3%)
    all_gather x4, waiting for transfers between devices, whole_rows(): return lax.all_gather(part, 'tensor', axis=1, tiled=True)  107 us
    reduce_scatter x4, waiting for transfers between devices, share_rows(): lax.psum_scatter(full.astype(jnp.bfloat16), 'tensor', scatter_dimension=1...  94.5 us
    unnamed x20, waiting for transfers between devices  75.5 us
    psum x1, blocking collectives, on_device(): head_sum, hidden_sum = lax.psum((head_grad, hidden_grad), 'dp')  62.1 us
    all_gather x1, waiting for transfers between devices, on_device(): lax.all_gather(reduce_weight.astype(jnp.bfloat16), 'dp', axis=1, tiled=True)  57.9 us
    all_gather x1, waiting for transfers between devices, on_device(): lax.all_gather(joint_weight.astype(jnp.bfloat16), 'dp', axis=0, tiled=True)  54.5 us
    all_gather x1, waiting for transfers between devices, on_device(): lax.all_gather(expand_weight.astype(jnp.bfloat16), 'dp', axis=0, tiled=True)  50.8 us
    psum x1, blocking collectives, on_device(): gain_sum, shift_sum = lax.psum((gain_grad, shift_grad), ('dp', 'tensor'))  40.8 us
  transfers between devices with their start and end apart: 16, of which 14 were waited for; matrix products, arithmetic and copies ran while one was open for 22% of the time, Pallas kernels for 0%

commit v1 on v0

--- a/solution.py
+++ b/solution.py
@@ -246,7 +246,13 @@
     owned = squares(joint_sum) + squares(expand_sum) + squares(output_sum) + squares(reduce_sum)
     shared = (squares(head_sum) + squares(hidden_sum)) / data_count
     everywhere = (squares(gain_sum) + squares(shift_sum)) / (data_count * split_count)
-    grad_norm = jnp.sqrt(lax.psum(owned + shared + everywhere, ("dp", "tensor")))
+
+    def direct_bench(array_here):
+        for src_i in ("tensor", "dp"):
+            array_here = lax.psum(array_here, axis_name=src_i)
+        return array_here
+
+    grad_norm = jnp.sqrt(direct_bench(owned + shared + everywhere))
     factor = clip_limit / jnp.maximum(grad_norm, clip_limit)
     joint_state = adamw_step(
         joint_weight, joint_sum, joint_moment, joint_square, factor, matrix_rate, decay_rate

time: 859 us -> 855 us (level)
    psum x1 -> x2, blocking collectives: 39.4 us -> 35.5 us  [direct_bench(): array_here = lax.psum(array_here, axis_name=src_i)]
where the time goes in v1:
time: 855 us; the launch traced here: 850 us
  waiting for transfers between devices  442 us (52%)
  blocking collectives  138 us (16%)
  matrix products  124 us (15%)
  other arithmetic  79.5 us (9%)
  local copies, waits for them, and re-layouts  40.6 us (5%)
  between operations  22.7 us (3%)
    all_gather x4, waiting for transfers between devices, whole_rows(): return lax.all_gather(part, 'tensor', axis=1, tiled=True)  107 us
    reduce_scatter x4, waiting for transfers between devices, share_rows(): lax.psum_scatter(full.astype(jnp.bfloat16), 'tensor', scatter_dimension=1...  94.5 us
    unnamed x20, waiting for transfers between devices  75.4 us
    psum x1, blocking collectives, on_device(): head_sum, hidden_sum = lax.psum((head_grad, hidden_grad), 'dp')  62.1 us
    all_gather x1, waiting for transfers between devices, on_device(): lax.all_gather(reduce_weight.astype(jnp.bfloat16), 'dp', axis=1, tiled=True)  57.9 us
    all_gather x1, waiting for transfers between devices, on_device(): lax.all_gather(joint_weight.astype(jnp.bfloat16), 'dp', axis=0, tiled=True)  54.5 us
    all_gather x1, waiting for transfers between devices, on_device(): lax.all_gather(expand_weight.astype(jnp.bfloat16), 'dp', axis=0, tiled=True)  50.8 us
    psum x1, blocking collectives, on_device(): gain_sum, shift_sum = lax.psum((gain_grad, shift_grad), ('dp', 'tensor'))  40.8 us
  transfers between devices with their start and end apart: 16, of which 14 were waited for; matrix products, arithmetic and copies ran while one was open for 22% of the time, Pallas kernels for 0%

profile of v1, /device:TPU:0, one launch (start us, length us, event | category | flops | bytes accessed | tf_op | source)
XLA Modules:
  0.0 849.6 jit_solution(4723418292910857077)
XLA Ops:
  17.5 29.0 %all-gather.9.cloned.1.call-done = bf16[1,736,1152]{2,1,0:T(8,128)(2,1)} async-done(((bf16[1,368,1152]{2,1,0:T(8,128)(2,1)}), bf16[1,736,1152]{2,1,0:T(8,128)(2,1)}) %all-gather.9.cloned.1.call-update) | async-done | bytes 1695760 | tf_op jit(solution)/shard_map/all_gather | solution.py:29
  46.5 54.5 %all-gather.11.cloned.1.call-done = bf16[1152,3,576]{2,0,1:T(8,128)(2,1)} async-done(((bf16[72,3,576]{2,0,1:T(8,128)(2,1)}), bf16[1152,3,576]{2,0,1:T(8,128)(2,1)}) %all-gather.11.cloned.1.call-update) | async-done | bytes 3981328 | tf_op jit(solution)/shard_map/all_gather | solution.py:181
  101.0 6.4 add_convert_fusion
  107.7 8.6 %fusion = (f32[8,736]{1,0:T(8,128)S(1)}, f32[8,736,736]{1,2,0:T(8,128)}) fusion(pred[736]{0:T(1024)(128)(4,1)S(1)} %iota_compare_fusion, bf16[736,8,72]{0,2,1:T(8,128)(2,1)S(1)} %bitcast.96, bf16[736,8,72]{0,2,1:T(8,128)(2,1)S(1)} %bitcast.94), kind=kOutput, calls=%fused_computation.5 | convolution fusion | flops 637028608 | bytes 19054304 | tf_op jit(solution)/shard_map/while/body/eval_jaxpr/qhd,khd->hqk/dot_general | solution.py:55
  116.3 10.0 %exponential_reduce_fusion = f32[8,736]{1,0:T(8,128)S(1)} fusion(f32[8,736,736]{1,2,0:T(8,128)} %get-tuple-element.122, f32[8,736]{1,0:T(8,128)S(1)} %get-tuple-element.121, pred[736]{0:T(1024)(128)(4,1)S(1)} %iota_compare_fusion), kind=kLoop, calls=%fused_computation.3 | loop fusion | flops 17328384 | bytes 17382112 | tf_op jit(solution)/shard_map/while/body/eval_jaxpr/reduce_sum | solution.py:66
  126.3 8.2 fusion.1
  146.9 25.5 %reduce-scatter.17.cloned.1.call-done = bf16[1,368,1152]{2,1,0:T(8,128)(2,1)} async-done(((bf16[1,736,1152]{2,1,0:T(8,128)(2,1)}), bf16[1,368,1152]{2,1,0:T(8,128)(2,1)}) %reduce-scatter.17.cloned.1.call-update) | async-done | bytes 847888 | tf_op jit(solution)/shard_map/reduce_scatter | solution.py:33
  179.3 50.8 %all-gather.17.cloned.1.call-done = bf16[1152,2152]{1,0:T(8,128)(2,1)} async-done(((bf16[72,2152]{1,0:T(8,128)(2,1)}), bf16[1152,2152]{1,0:T(8,128)(2,1)}) %all-gather.17.cloned.1.call-update) | async-done | bytes 4958224 | tf_op jit(solution)/shard_map/all_gather | solution.py:182
  230.1 29.2 %all-gather.15.cloned.1.call-done = bf16[1,736,1152]{2,1,0:T(8,128)(2,1)} async-done(((bf16[1,368,1152]{2,1,0:T(8,128)(2,1)}), bf16[1,736,1152]{2,1,0:T(8,128)(2,1)}) %all-gather.15.cloned.1.call-update) | async-done | bytes 1695760 | tf_op jit(solution)/shard_map/all_gather | solution.py:29
  259.4 10.1 %fusion.38 = f32[736,2152]{1,0:T(8,128)} fusion(bf16[1152,2152]{1,0:T(8,128)(2,1)} %all-gather.17.cloned.1.call-done, bf16[1,736,1152]{2,1,0:T(8,128)(2,1)} %all-gather.15.cloned.1.call-done), kind=kOutput, calls=%fused_computation.72 | convolution fusion | flops 3649241088 | bytes 12989440 | tf_op jit(solution)/shard_map/bsd,df->bsf/dot_general | solution.py:115
  269.5 20.1 %all-gather.21.cloned.1.call-done = bf16[1,736,1152]{2,1,0:T(8,128)(2,1)} async-done(((bf16[1,368,1152]{2,1,0:T(8,128)(2,1)}), bf16[1,736,1152]{2,1,0:T(8,128)(2,1)}) %all-gather.21.cloned.1.call-update) | async-done | bytes 1695760 | tf_op jit(solution)/shard_map/all_gather | solution.py:29
  289.6 57.9 %all-gather.19.cloned.1.call-done = bf16[2152,1152]{0,1:T(8,128)(2,1)} async-done(((bf16[2152,72]{0,1:T(8,128)(2,1)}), bf16[2152,1152]{0,1:T(8,128)(2,1)}) %all-gather.19.cloned.1.call-update) | async-done | bytes 4958224 | tf_op jit(solution)/shard_map/all_gather | solution.py:186
  347.5 11.3 %convert_reduce_fusion = (f32[2152]{0:T(1024)S(1)}, bf16[736,2152]{1,0:T(8,128)(2,1)S(1)}) fusion(f32[736,2152]{1,0:T(8,128)} %fusion.38, f32[2152]{0:T(1024)S(1)} %copy-done.46, bf16[2152,1152]{0,1:T(8,128)(2,1)} %all-gather.19.cloned.1.call-done, bf16[1,736,1152]{2,1,0:T(8,128)(2,1)} %all-gather.21.cloned.1.call-done), kind=kOutput, calls=%fused_computation.18 | convolution fusion | flops 3685668096 | bytes 16174400 | tf_op jit(solution)/shard_map/bsd,fd->bsf/dot_general | solution.py:199
  360.5 8.2 fusion.13
  368.9 11.1 %fusion.12 = bf16[1,736,1152]{2,1,0:T(8,128)(2,1)} fusion(bf16[2152,1152]{0,1:T(8,128)(2,1)} %all-gather.19.cloned.1.call-done, f32[736,2152]{1,0:T(8,128)} %fusion.38, f32[2152]{0:T(1024)S(1)} %copy-done.46), kind=kOutput, calls=%fused_computation.31 | convolution fusion | flops 3665927680 | bytes 12998048 | tf_op jit(solution)/shard_map/bsf,fd->bsd/dot_general | solution.py:121
  380.1 14.7 %reduce-scatter.21.cloned.1.call-done = bf16[1,368,1152]{2,1,0:T(8,128)(2,1)} async-done(((bf16[1,736,1152]{2,1,0:T(8,128)(2,1)}), bf16[1,368,1152]{2,1,0:T(8,128)(2,1)}) %reduce-scatter.21.cloned.1.call-update) | async-done | bytes 847888 | tf_op jit(solution)/shard_map/reduce_scatter | solution.py:33
  396.8 27.5 %reduce-scatter.19.cloned.1.call-done = bf16[1,368,1152]{2,1,0:T(8,128)(2,1)} async-done(((bf16[1,736,1152]{2,1,0:T(8,128)(2,1)}), bf16[1,368,1152]{2,1,0:T(8,128)(2,1)}) %reduce-scatter.19.cloned.1.call-update) | async-done | bytes 847888 | tf_op jit(solution)/shard_map/reduce_scatter | solution.py:33
  429.0 28.7 %all-gather.23.cloned.1.call-done = bf16[1,736,1152]{2,1,0:T(8,128)(2,1)} async-done(((bf16[1,368,1152]{2,1,0:T(8,128)(2,1)}), bf16[1,736,1152]{2,1,0:T(8,128)(2,1)}) %all-gather.23.cloned.1.call-update) | async-done | bytes 1695760 | tf_op jit(solution)/shard_map/all_gather | solution.py:29
  462.4 10.1 %convolution_convert_fusion = bf16[2152,1152]{0,1:T(8,128)(2,1)} fusion(bf16[1,736,1152]{2,1,0:T(8,128)(2,1)} %all-gather.21.cloned.1.call-done, f32[736,2152]{1,0:T(8,128)} %fusion.38, f32[2152]{0:T(1024)S(1)} %copy-done.46), kind=kOutput, calls=%fused_computation.6 | convolution fusion | flops 3667558912 | bytes 12998048 | tf_op jit(solution)/shard_map/bsf,bsd->fd/dot_general | solution.py:198
  472.6 9.1 %convolution_convert_fusion.1 = bf16[1152,2152]{1,0:T(8,128)(2,1)} fusion(bf16[736,2152]{1,0:T(8,128)(2,1)} %copy-done.47, bf16[1,736,1152]{2,1,0:T(8,128)(2,1)} %all-gather.15.cloned.1.call-done), kind=kOutput, calls=%fused_computation.7 | convolution fusion | flops 3651720192 | bytes 9821696 | tf_op jit(solution)/shard_map/bsd,bsf->df/dot_general | solution.py:203
  485.0 6.4 convolution_convert_fusion.7
  491.4 13.2 %multiply_reduce_fusion = (f32[8,736]{1,0:T(8,128)S(1)}, f32[8,736,736]{1,2,0:T(8,128)}) fusion(f32[8,736,736]{1,2,0:T(8,128)} %get-tuple-element.122, f32[8,736]{1,0:T(8,128)S(1)} %log_add_fusion, pred[736]{0:T(1024)(128)(4,1)S(1)} %iota_compare_fusion, bf16[736,8,72]{0,2,1:T(8,128)(2,1)S(1)} %bitcast.108, bf16[736,8,72]{0,2,1:T(8,128)(2,1)S(1)} %bitcast.93), kind=kOutput, calls=%fused_computation.1 | convolution fusion | flops 645695744 | bytes 36412128 | tf_op jit(solution)/shard_map/while/body/eval_jaxpr/qhd,khd->hqk/dot_general | solution.py:84
  504.6 13.0 %multiply_convert_fusion = bf16[8,736,736]{1,2,0:T(8,128)(2,1)S(1)} fusion(f32[8,736,736]{1,2,0:T(8,128)} %get-tuple-element.124, f32[8,736,736]{1,2,0:T(8,128)} %get-tuple-element.122, f32[8,736]{1,0:T(8,128)S(1)} %get-tuple-element.123, f32[8,736]{1,0:T(8,128)S(1)} %log_add_fusion, pred[736]{0:T(1024)(128)(4,1)S(1)} %iota_compare_fusion), kind=kLoop, calls=%fused_computation | loop fusion | flops 26001408 | bytes 43383520 | tf_op jit(solution)/shard_map/while/body/eval_jaxpr/convert_element_type | solution.py:86
  528.8 6.3 convolution_convert_fusion.2
  535.2 18.2 %copy.70 = bf16[1152,3,576]{2,1,0:T(4,128)(2,1)} copy(bf16[1152,3,576]{2,0,1:T(8,128)(2,1)S(1)} %convolution_convert_fusion.2) | data formatting | bytes 7962624
  553.4 12.4 %reshape.392 = bf16[1152,1728]{1,0:T(8,128)(2,1)} reshape(bf16[1152,3,576]{2,1,0:T(4,128)(2,1)} %copy.70) | data formatting | bytes 7962624
  568.3 62.1 %all-reduce.4 = (f32[2,576]{1,0:T(2,128)S(1)}, f32[2152]{0:T(1024)S(1)}) all-reduce(f32[2,576]{1,0:T(2,128)S(1)} %convert_reduce_fusion.1, f32[2152]{0:T(1024)S(1)} %get-tuple-element.125), channel_id=1, replica_groups=mesh['dp'=16,'tensor'=2] {'dp'}, use_global_device_ids=true, to_apply=%region_24.25 | all-reduce | flops 3304 | bytes 26432 | tf_op jit(solution)/shard_map/psum | solution.py:243
  636.3 47.3 %reduce-scatter.27.cloned.1.call-done = bf16[72,2152]{1,0:T(8,128)(2,1)} async-done(((bf16[1152,2152]{1,0:T(8,128)(2,1)}), bf16[72,2152]{1,0:T(8,128)(2,1)}) %reduce-scatter.27.cloned.1.call-update) | async-done | bytes 309904
  685.4 26.8 %reduce-scatter.23.cloned.1.call-done = bf16[1,368,1152]{2,1,0:T(8,128)(2,1)} async-done(((bf16[1,736,1152]{2,1,0:T(8,128)(2,1)}), bf16[1,368,1152]{2,1,0:T(8,128)(2,1)}) %reduce-scatter.23.cloned.1.call-update) | async-done | bytes 847888 | tf_op jit(solution)/shard_map/reduce_scatter | solution.py:33
  717.9 40.8 %all-reduce.3 = (f32[2,1152]{1,0:T(2,128)S(1)}, f32[4,1152]{1,0:T(4,128)S(1)}) all-reduce(f32[2,1152]{1,0:T(2,128)S(1)} %pad_maximum_fusion.6, f32[4,1152]{1,0:T(4,128)S(1)} %pad_maximum_fusion.4), channel_id=1, replica_groups=mesh['dp'=16,'tensor'=2] {'dp','tensor'}, use_global_device_ids=true, to_apply=%region_31.32 | all-reduce | flops 6912 | bytes 55296 | tf_op jit(solution)/shard_map/psum | solution.py:242
  761.4 27.2 %reduce-scatter.25.cloned.1.call-done = bf16[72,1728]{1,0:T(8,128)(2,1)} async-done(((bf16[1152,1728]{1,0:T(8,128)(2,1)}), bf16[72,1728]{1,0:T(8,128)(2,1)}) %reduce-scatter.25.cloned.1.call-update) | async-done | bytes 248848
  798.5 30.1 %psum.47 = f32[]{:T(128)} all-reduce(f32[]{:T(128)} %psum.46), channel_id=1, replica_groups=mesh['dp'=16,'tensor'=2] {'dp'}, use_global_device_ids=true, to_apply=%region_40.41 | all-reduce | flops 1 | bytes 8 | tf_op jit(solution)/shard_map/psum | solution.py:252
  (203 shorter events, 91.9 us)
Async XLA Ops:
  7.2 39.3 %all-gather.9.cloned.1.call-start = ((), (), s32[]{:S(2)}) async-start(), calls=%async_computation.8 | async-start | bytes 2543616 | tf_op jit(solution)/shard_map/all_gather | solution.py:29
  8.7 98.8 %copy-start.35 = (f32[368]{0:T(512)}, f32[368]{0:T(512)S(1)}, u32[]{:S(2)}) copy-start(f32[368]{0:T(512)S(1)} %broadcast_multiply_fusion.1) | copy-start | bytes 4420
  10.8 96.6 %copy-start.38 = (f32[368]{0:T(512)}, f32[368]{0:T(512)S(1)}, u32[]{:S(2)}) copy-start(f32[368]{0:T(512)S(1)} %fusion.61) | copy-start | bytes 4420
  11.6 95.8 %copy-start.30 = (f32[1152]{0:T(1024)}, f32[1152]{0:T(1024)S(1)}, u32[]{:S(2)}) copy-start(f32[1152]{0:T(1024)S(1)} %get-tuple-element.75) | copy-start | bytes 13828
  15.0 86.0 %all-gather.11.cloned.1.call-start = ((), (), s32[]{:S(2)}) async-start(), calls=%async_computation.9 | async-start | bytes 4700160 | tf_op jit(solution)/shard_map/all_gather | solution.py:181
  15.9 125.8 %all-gather.13.cloned.1.call-start = ((), (), s32[]{:S(2)}) async-start(), calls=%async_computation.10 | async-start | bytes 1566720 | tf_op jit(solution)/shard_map/all_gather | solution.py:185
  16.6 155.8 %reduce-scatter.17.cloned.1.call-start = ((), (), s32[]{:S(2)}) async-start(), calls=%async_computation.11 | async-start | bytes 2543616 | tf_op jit(solution)/shard_map/reduce_scatter | solution.py:33
  146.0 84.2 %all-gather.17.cloned.1.call-start = ((), (), s32[]{:S(2)}) async-start(), calls=%async_computation.13 | async-start | bytes 5326848 | tf_op jit(solution)/shard_map/all_gather | solution.py:182
  146.8 112.6 %all-gather.15.cloned.1.call-start = ((), (), s32[]{:S(2)}) async-start(), calls=%async_computation.12 | async-start | bytes 2543616 | tf_op jit(solution)/shard_map/all_gather | solution.py:29
  177.2 112.5 %all-gather.21.cloned.1.call-start = ((), (), s32[]{:S(2)}) async-start(), calls=%async_computation.16 | async-start | bytes 2543616 | tf_op jit(solution)/shard_map/all_gather | solution.py:29
  177.9 169.6 %all-gather.19.cloned.1.call-start = ((), (), s32[]{:S(2)}) async-start(), calls=%async_computation.14 | async-start | bytes 5326848 | tf_op jit(solution)/shard_map/all_gather | solution.py:186
  178.7 168.8 %copy-start.46 = (f32[2152]{0:T(1024)S(1)}, f32[2152]{0:T(1024)}, u32[]{:S(2)}) copy-start(f32[2152]{0:T(1024)} %param.51) | copy-start | bytes 25828
  178.8 216.0 %reduce-scatter.21.cloned.1.call-start = ((), (), s32[]{:S(2)}) async-start(), calls=%async_computation.17 | async-start | bytes 2543616 | tf_op jit(solution)/shard_map/reduce_scatter | solution.py:33
  368.7 55.7 %reduce-scatter.19.cloned.1.call-start = ((), (), s32[]{:S(2)}) async-start(), calls=%async_computation.15 | async-start | bytes 2543616 | tf_op jit(solution)/shard_map/reduce_scatter | solution.py:33
  380.0 77.7 %all-gather.23.cloned.1.call-start = ((), (), s32[]{:S(2)}) async-start(), calls=%async_computation.18 | async-start | bytes 2543616 | tf_op jit(solution)/shard_map/all_gather | solution.py:29
  428.9 204.0 %reduce-scatter.29.cloned.1.call-start = ((), (), s32[]{:S(2)}) async-start(), calls=%async_computation.22 | async-start | bytes 1566720
  462.2 172.3 %reduce-scatter.31.cloned.1.call-start = ((), (), s32[]{:S(2)}) async-start(), calls=%async_computation.23 | async-start | bytes 5326848
  472.5 211.1 %reduce-scatter.27.cloned.1.call-start = ((), (), s32[]{:S(2)}) async-start(), calls=%async_computation.21 | async-start | bytes 5326848
  481.7 230.4 %reduce-scatter.23.cloned.1.call-start = ((), (), s32[]{:S(2)}) async-start(), calls=%async_computation.19 | async-start | bytes 2543616 | tf_op jit(solution)/shard_map/reduce_scatter | solution.py:33
  528.6 259.9 %reduce-scatter.25.cloned.1.call-start = ((), (), s32[]{:S(2)}) async-start(), calls=%async_computation.20 | async-start | bytes 4386816
  565.8 146.3 %copy-start.31 = (f32[1152]{0:T(1024)S(1)}, f32[1152]{0:T(1024)}, u32[]{:S(2)}) copy-start(f32[1152]{0:T(1024)} %copy-done.30) | copy-start | bytes 13828
  565.9 146.3 %copy-start.36 = (f32[368]{0:T(512)S(1)}, f32[368]{0:T(512)}, u32[]{:S(2)}) copy-start(f32[368]{0:T(512)} %copy-done.35) | copy-start | bytes 4420
  567.9 146.0 %copy-start.45 = (f32[368]{0:T(512)S(1)}, f32[368]{0:T(512)}, u32[]{:S(2)}) copy-start(f32[368]{0:T(512)} %copy-done.44) | copy-start | bytes 4420
  568.0 146.0 %copy-start.39 = (f32[368]{0:T(512)S(1)}, f32[368]{0:T(512)}, u32[]{:S(2)}) copy-start(f32[368]{0:T(512)} %copy-done.38) | copy-start | bytes 4420
  568.0 148.0 %copy-start.10 = (bf16[1,368,1152]{2,1,0:T(8,128)(2,1)S(1)}, bf16[1,368,1152]{2,1,0:T(8,128)(2,1)}, u32[]{:S(2)}) copy-start(bf16[1,368,1152]{2,1,0:T(8,128)(2,1)} %param.28) | copy-start | bytes 2543620
  716.0 113.3 %copy-start.41 = (f32[2,576]{1,0:T(2,128)S(1)}, f32[2,576]{1,0:T(2,128)}, u32[]{:S(2)}) copy-start(f32[2,576]{1,0:T(2,128)} %param.48) | copy-start | bytes 13828
  716.0 114.6 %copy-start.37 = (f32[2,1152]{1,0:T(2,128)S(1)}, f32[2,1152]{1,0:T(2,128)}, u32[]{:S(2)}) copy-start(f32[2,1152]{1,0:T(2,128)} %param.42) | copy-start | bytes 27652
  716.0 117.3 %copy-start.34 = (f32[4,1152]{1,0:T(4,128)S(1)}, f32[4,1152]{1,0:T(4,128)}, u32[]{:S(2)}) copy-start(f32[4,1152]{1,0:T(4,128)} %param.45) | copy-start | bytes 55300
  716.1 117.3 %copy-start.42 = (f32[4,1152]{1,0:T(4,128)S(1)}, f32[4,1152]{1,0:T(4,128)}, u32[]{:S(2)}) copy-start(f32[4,1152]{1,0:T(4,128)} %param.46) | copy-start | bytes 55300
  716.1 117.3 %copy-start.43 = (f32[4,1152]{1,0:T(4,128)S(1)}, f32[4,1152]{1,0:T(4,128)}, u32[]{:S(2)}) copy-start(f32[4,1152]{1,0:T(4,128)} %param.47) | copy-start | bytes 55300
  760.0 77.2 %copy-start.32 = (f32[576,72]{0,1:T(8,128)S(1)}, f32[576,72]{0,1:T(8,128)}, u32[]{:S(2)}) copy-start(f32[576,72]{0,1:T(8,128)} %param.34) | copy-start | bytes 497668
  760.0 77.2 %copy-start.33 = (f32[576,72]{0,1:T(8,128)S(1)}, f32[576,72]{0,1:T(8,128)}, u32[]{:S(2)}) copy-start(f32[576,72]{0,1:T(8,128)} %param.35) | copy-start | bytes 497668
  (34 other events, 372.3 us)
Sparse Core Ops, SparseCore 0:
  15.2 31.2 all-gather.8
  49.3 51.7 all-gather.10
  103.8 37.8 all-gather.12
  146.1 26.2 reduce-scatter.16
  175.2 54.8 all-gather.16
  232.2 27.1 all-gather.14
  261.0 28.5 all-gather.20
  292.6 54.9 all-gather.18
  368.8 25.9 reduce-scatter.20
  396.9 27.4 reduce-scatter.18
  429.1 28.5 all-gather.22
  462.3 58.7 reduce-scatter.28
  525.6 77.2 reduce-scatter.30
  606.7 76.8 reduce-scatter.26
  685.8 26.2 reduce-scatter.22
  715.9 72.6 reduce-scatter.24
